TPU v7x, 32 devices: a whole 2x2x4 slice. The times are simulated.
32 devices in a mesh: grp: 2 (over x), tm: 16 (over z, y, core).
Axes of the slice: x: 2, y: 2, z: 4, core: 2. Of those that a mesh axis runs over, the one named last changes fastest.
Arguments:
- raw_frames: bfloat16 [96, 256, 256], P(('grp', 'tm')), parts along dimension 0, may hold values from 0 to 2
- angle_index: int32 [96], P('grp'), parts along dimension 0, may hold values from 0 to 2
- phase_index: int32 [96], P('grp'), parts along dimension 0, may hold values from 0 to 2
- band_shift: int32 [6, 2], P('grp'), parts along dimension 0, may hold values from 16 to 127, as said below
Outputs:
- denoised: float32 [32, 512, 512], P('grp', 'tm'), parts along dimension 0
There are 2 independent parts, one for each index of `grp`. A program takes and returns all parts, laid end to end along the dimension named above; each array names one. Nothing has to cross between parts.
Inputs may be any that keep to these rules, and one draw needn't show every extreme that they name: `band_shift`: offsets are in cycles across the 512-pixel grid.
All inputs are finite; a program needn't handle non-finite values.
Results may differ from a plain program's by a relative error of at most 0.0049.
Values may be sent and summed in bfloat16 or wider, within the bound.
No kernel may reach another device: no remote copies, remote signals or barrier semaphores. Data moves between devices by JAX's collectives and lax.ppermute only.
A program may use at most 64 MiB of HBM per device.

v0:
```python
import jax
import jax.numpy as jnp
from jax import lax
from jax.sharding import PartitionSpec as P

SWEEPS = 2


TERM_WEIGHTS = (1.0, 1.0, 1.0, 2.0, 2.0, 2.0)
STEP_SIZE = 0.01
THRESHOLD = 2.0


def with_halo(cells, sides, width):
    for axis, dim in sides:
        count = lax.axis_size(axis)
        ends = count - 1
        head = lax.slice_in_dim(cells, 0, width, axis=dim)
        tail = lax.slice_in_dim(cells, cells.shape[dim] - width, cells.shape[dim], axis=dim)
        cells = jnp.concatenate(
            [
                lax.ppermute(tail, axis, [(i, (i + 1) % count) for i in range(ends)]),
                cells,
                lax.ppermute(head, axis, [((i + 1) % count, i) for i in range(ends)]),
            ],
            axis=dim,
        )
    return cells


def half_table(coarse):
    row_index = lax.broadcasted_iota(jnp.int32, (coarse, coarse), 0)
    col_index = lax.broadcasted_iota(jnp.int32, (coarse, coarse), 1)
    offset = row_index - col_index
    parity = 1.0 - 2.0 * (offset % 2).astype(jnp.float32)
    angle_arg = jnp.pi * (offset.astype(jnp.float32) + 0.5) / coarse
    return (parity / (coarse * jnp.tan(angle_arg))).astype(jnp.bfloat16)


def wiener_table(grid_width):
    row_index = lax.broadcasted_iota(jnp.int32, (grid_width, grid_width), 0)
    col_index = lax.broadcasted_iota(jnp.int32, (grid_width, grid_width), 1)
    distance = jnp.abs(row_index - col_index)
    distance = jnp.minimum(distance, grid_width - distance)
    taps_value = -0.01 * jnp.power(0.98, (distance - 1).astype(jnp.float32))
    return jnp.where(distance == 0, 1.0, taps_value).astype(jnp.bfloat16)


def pattern_weight(angles, phases, band_shift, grid_width):
    angle_hit = angles[:, None] == jnp.arange(3, dtype=jnp.int32)[None, :]
    shift_rows = jnp.sum(jnp.where(angle_hit, band_shift[None, :, 0], 0), axis=1)
    shift_cols = jnp.sum(jnp.where(angle_hit, band_shift[None, :, 1], 0), axis=1)
    line_pos = jnp.arange(grid_width, dtype=jnp.int32)
    row_cycle = shift_rows[:, None] * line_pos[None, :] % grid_width
    col_cycle = shift_cols[:, None] * line_pos[None, :] % grid_width
    row_turn = 2.0 * jnp.pi * row_cycle.astype(jnp.float32) / grid_width
    col_turn = (
        2.0
        * jnp.pi
        * ((3 * col_cycle - phases[:, None] * grid_width).astype(jnp.float32) / (3.0 * grid_width))
    )
    row_cos = jnp.cos(row_turn)[:, :, None]
    row_sin = jnp.sin(row_turn)[:, :, None]
    col_cos = jnp.cos(col_turn)[:, None, :]
    col_sin = jnp.sin(col_turn)[:, None, :]
    return (1.0 + 2.0 * (row_cos * col_cos - row_sin * col_sin)) / 3.0


def weighted_frames(raw_block, angles, phases, band_shift):
    frame_count = raw_block.shape[0]
    coarse = raw_block.shape[1]
    half_step = half_table(coarse)
    odd_rows = jnp.einsum(
        "ki,fij->fkj", half_step, raw_block, preferred_element_type=jnp.float32
    ).astype(jnp.bfloat16)
    rows_done = jnp.stack([raw_block, odd_rows], axis=2).reshape(frame_count, 2 * coarse, coarse)
    identity = jnp.eye(coarse, dtype=jnp.bfloat16)
    spread = jnp.stack([identity, half_step], axis=1).reshape(2 * coarse, coarse)
    upsampled = jnp.einsum("fij,kj->fik", rows_done, spread, preferred_element_type=jnp.float32)
    return pattern_weight(angles, phases, band_shift, 2 * coarse) * upsampled


def shift_ahead(field, axis):
    count = field.shape[axis]
    tail_zero = jnp.zeros_like(lax.slice_in_dim(field, 0, 1, axis=axis))
    return jnp.concatenate([lax.slice_in_dim(field, 1, count, axis=axis), tail_zero], axis)


def shift_behind(field, axis):
    count = field.shape[axis]
    head_zero = jnp.zeros_like(lax.slice_in_dim(field, 0, 1, axis=axis))
    return jnp.concatenate([head_zero, lax.slice_in_dim(field, 0, count - 1, axis=axis)], axis)


def second_diff(field, axis):
    return shift_ahead(field, axis) - 2.0 * field + shift_behind(field, axis)


def back_diff(field, axis):
    return field - shift_behind(field, axis)


def hessian_terms(field):
    rise_rows = shift_ahead(field, 1) - field
    time_rise = shift_ahead(field, 0) - field
    return (
        second_diff(field, 2),
        second_diff(field, 1),
        second_diff(field, 0),
        shift_ahead(rise_rows, 2) - rise_rows,
        shift_ahead(time_rise, 2) - time_rise,
        shift_ahead(rise_rows, 0) - rise_rows,
    )


def adjoint_sum(carried):
    carry_xx, carry_yy, carry_tt, carry_xy, carry_xt, carry_yt = carried
    result = TERM_WEIGHTS[0] * second_diff(carry_xx, 2)
    result = result + TERM_WEIGHTS[1] * second_diff(carry_yy, 1)
    result = result + TERM_WEIGHTS[2] * second_diff(carry_tt, 0)
    result = result + TERM_WEIGHTS[3] * back_diff(back_diff(carry_xy, 2), 1)
    result = result + TERM_WEIGHTS[4] * back_diff(back_diff(carry_xt, 2), 0)
    result = result + TERM_WEIGHTS[5] * back_diff(back_diff(carry_yt, 1), 0)
    return result


def shards(raw_frames, angle_index, phase_index, band_shift):
    raw_count = raw_frames.shape[0]
    out_count = raw_count // 3
    fine_width = 2 * raw_frames.shape[1]
    position = lax.axis_index("tm")
    padded_angle = jnp.pad(angle_index, (3, 3))
    padded_phase = jnp.pad(phase_index, (3, 3))
    borrowed = with_halo(raw_frames, (("tm", 0),), 3)
    angles = lax.dynamic_slice_in_dim(padded_angle, position * raw_count, raw_count + 6, 0)
    phases = lax.dynamic_slice_in_dim(padded_phase, position * raw_count, raw_count + 6, 0)
    weighted = weighted_frames(borrowed, angles, phases, band_shift)
    groups = weighted.reshape(out_count + 2, 3, fine_width, fine_width).sum(axis=1)
    summed = (groups[:-2] + groups[1:-1] + groups[2:]).astype(jnp.bfloat16)
    wiener = wiener_table(fine_width)
    filtered = jnp.einsum("ab,kbc->kac", wiener, summed, preferred_element_type=jnp.float32).astype(
        jnp.bfloat16
    )
    frames = jnp.einsum("kab,cb->kac", filtered, wiener, preferred_element_type=jnp.float32).astype(
        jnp.bfloat16
    )
    tm_count = lax.axis_size("tm")
    block_rows = fine_width // tm_count
    reach = 2 * SWEEPS
    window_rows = block_rows + 2 * reach
    piece_count = -(-(2 * reach) // block_rows) + 1
    tall = jnp.pad(frames, ((0, 0), (reach, (piece_count - 1) * block_rows), (0, 0)))
    pieces = [
        tall[:, piece * block_rows : piece * block_rows + fine_width].reshape(
            out_count, tm_count, block_rows, fine_width
        )
        for piece in range(piece_count)
    ]
    windows = jnp.concatenate(pieces, axis=2)[:, :, :window_rows]
    deep_frames = lax.all_to_all(windows, "tm", split_axis=1, concat_axis=0, tiled=True)
    guide_field = deep_frames.reshape(out_count * tm_count, window_rows, fine_width).astype(
        jnp.float32
    )
    row_index = (
        position * block_rows - reach + lax.broadcasted_iota(jnp.int32, (1, window_rows, 1), 1)
    )
    row_valid = ((row_index >= 0) & (row_index < fine_width)).astype(jnp.float32)
    estimate = guide_field
    dual_terms = tuple((jnp.zeros_like(guide_field) for _ in range(6)))
    for sweep_index in range(SWEEPS):
        terms = hessian_terms(estimate)
        fresh = tuple(
            (
                jnp.clip(term + dual, -THRESHOLD, THRESHOLD) * row_valid
                for term, dual in zip(terms, dual_terms)
            )
        )
        carried = tuple((2.0 * new_dual - dual for new_dual, dual in zip(fresh, dual_terms)))
        estimate = (
            estimate - STEP_SIZE * (estimate - guide_field + adjoint_sum(carried))
        ) * row_valid
        dual_terms = fresh
    return estimate[:, reach : reach + block_rows]


def solution(mesh):
    return jax.shard_map(
        shards,
        mesh=mesh,
        in_specs=(P(("grp", "tm"), None, None), P("grp"), P("grp"), P("grp", None)),
        out_specs=P("grp", "tm", None),
        check_vma=False,
    )
```

profile of v0, /device:TPU:0, one launch (start us, length us, event | category | flops | bytes accessed | tf_op | source)
XLA Modules:
  0.0 112.0 jit_solution(10099077840732901685)
XLA Ops:
  0.0 2.5 %collective-permute-start = (bf16[3,256,256]{2,1,0:T(8,128)(2,1)}, bf16[3,256,256]{2,1,0:T(8,128)(2,1)S(1)}, u32[]{:S(2)}, u32[]{:S(2)}) collective-permute-start(bf16[3,256,256]{2,1,0:T(8,128)(2,1)} %param.4), channel_id=1, source_target_pairs={{0,1},{1,2},{2,3},{3,4},{4,5},{5,6},{6,7},{7,8},{8,9},{9,10},{10,1... | collective-permute-start | bytes 1179656 | tf_op jit(solution)/shard_map/ppermute | solution.py:22
  2.6 1.3 %collective-permute-start.1 = (bf16[3,256,256]{2,1,0:T(8,128)(2,1)}, bf16[3,256,256]{2,1,0:T(8,128)(2,1)S(1)}, u32[]{:S(2)}, u32[]{:S(2)}) collective-permute-start(bf16[3,256,256]{2,1,0:T(8,128)(2,1)} %param.4), channel_id=1, source_target_pairs={{1,0},{2,1},{3,2},{4,3},{5,4},{6,5},{7,6},{8,7},{9,8},{10,9},{11,1... | collective-permute-start | bytes 1179656 | tf_op jit(solution)/shard_map/ppermute | solution.py:24
  3.9 9.0 %fusion.35 = bf16[256,1,256]{2,1,0:T(2,128)(2,1)S(1)} fusion(), kind=kLoop, calls=%fused_computation.86 | loop fusion | flops 1376256 | bytes 131072 | tf_op jit(solution)/shard_map/convert_element_type | solution.py:37
  13.1 0.8 slice_bitcast_fusion.2
  13.8 0.6 pad_maximum_fusion.2
  15.3 1.5 %fusion = bf16[9,256,1,256]{3,1,0,2:T(8,128)(2,1)S(1)} fusion(bf16[9,256,256]{2,1,0:T(8,128)(2,1)S(1)} %constant_dynamic-update-slice_fusion), kind=kOutput, calls=%fused_computation.4 | convolution fusion | flops 303955968 | bytes 2359296 | tf_op jit(solution)/shard_map/ki,fij->fkj/dot_general | solution.py:73
  17.1 3.9 %copy.10 = bf16[9,256,2,256]{3,2,1,0:T(2,128)(2,1)} copy(bf16[9,256,2,256]{3,1,0,2:T(8,128)(2,1)S(1)} %pad_maximum_fusion) | data formatting | bytes 4718592 | tf_op jit(solution)/shard_map/stack | solution.py:76
  21.0 6.1 %reshape.258 = bf16[9,512,256]{2,1,0:T(8,128)(2,1)} reshape(bf16[9,256,2,256]{3,2,1,0:T(2,128)(2,1)} %copy.10) | data formatting | bytes 4718592 | tf_op jit(solution)/shard_map/reshape | solution.py:76
  27.1 6.2 %multiply_multiply_fusion = f32[9,512,512]{2,1,0:T(8,128)} fusion(f32[9,512]{1,0:T(8,128)S(1)} %get-tuple-element.60, f32[9,512]{1,0:T(8,128)S(1)} %get-tuple-element.66, f32[9,512]{1,0:T(8,128)S(1)} %get-tuple-element.59, f32[9,512]{1,0:T(8,128)S(1)} %get-tuple-element.65, bf16[9,512,256]{2,1,0:T(8,128)(2,1)} %reshape.258, bf16[512,256,1]{1,0,2:T(8,128)(2,1)S(1)} %reshape.266), kind=kOutput, calls=%fused_computation | convolution fusion | flops 1224474624 | bytes 12132352 | tf_op jit(solution)/shard_map/fij,kj->fik/dot_general | solution.py:79
  33.3 6.9 %reduce_sum.29 = f32[3,512,512]{2,1,0:T(8,128)} reduce(f32[3,3,512,512]{3,2,1,0:T(8,128)} %bitcast.77, f32[]{:T(128)} %constant.97.clone.1), dimensions={1}, to_apply=%region_2.3 | reduce | flops 1572864 | bytes 12582916 | tf_op jit(solution)/shard_map/reduce_sum | solution.py:138
  40.2 3.2 %fusion.2 = bf16[1,512,512]{2,1,0:T(8,128)(2,1)S(1)} fusion(f32[3,512,512]{2,1,0:T(8,128)} %reduce_sum.29), kind=kOutput, calls=%fused_computation.32 | convolution fusion | flops 543424512 | bytes 3670016 | tf_op jit(solution)/shard_map/kab,cb->kac/dot_general | solution.py:144
  43.5 0.9 pad_maximum_fusion.1
  44.4 9.3 %all-to-all-start = ((bf16[1,16,40,512]{3,2,0,1:T(8,128)(2,1)}), bf16[1,16,40,512]{3,2,0,1:T(8,128)(2,1)S(1)}, u32[]{:S(2)}, u32[]{:S(2)}) async-start(bf16[1,16,40,512]{3,2,0,1:T(8,128)(2,1)} %pad_maximum_fusion.1), calls=%async_computation | async-start | bytes 1310720 | tf_op jit(solution)/shard_map/all_to_all | solution.py:160
  53.7 16.5 %all-to-all-done = bf16[1,16,40,512]{3,2,0,1:T(8,128)(2,1)S(1)} async-done(((bf16[1,16,40,512]{3,2,0,1:T(8,128)(2,1)}), bf16[1,16,40,512]{3,2,0,1:T(8,128)(2,1)S(1)}, u32[]{:S(2)}, u32[]{:S(2)}) %all-to-all-start) | async-done | bytes 655392 | tf_op jit(solution)/shard_map/all_to_all | solution.py:160
  71.3 1.6 %fusion.95 = (f32[16,40,511]{2,1,0:T(8,128)S(1)}, f32[16,40,511]{2,1,0:T(8,128)}) fusion(f32[16,40,512]{2,1,0:T(8,128)S(1)} %get-tuple-element.55), kind=kLoop, calls=%fused_computation.157 | loop fusion | bytes 5232640 | tf_op jit(solution)/shard_map/slice | solution.py:86
  72.9 1.1 %slice_bitcast_fusion = f32[15,40,512]{2,1,0:T(8,128)} fusion(f32[1,16,40,512]{3,2,0,1:T(8,128)S(1)} %get-tuple-element.54), kind=kLoop, calls=%fused_computation.35 | loop fusion | bytes 2457600 | tf_op jit(solution)/shard_map/slice | solution.py:92
  74.0 1.1 %slice_bitcast_fusion.1 = f32[15,40,512]{2,1,0:T(8,128)} fusion(f32[1,16,40,512]{3,2,1,0:T(8,128)S(1)} %get-tuple-element.56), kind=kLoop, calls=%fused_computation.36 | loop fusion | bytes 2457600 | tf_op jit(solution)/shard_map/slice | solution.py:86
  75.3 3.8 %broadcast_multiply_fusion.5 = (f32[16,40,512]{2,1,0:T(8,128)S(1)}, f32[16,40,512]{2,1,0:T(8,128)S(1)}, f32[16,40,512]{2,1,0:T(8,128)S(1)}, f32[16,40,512]{2,1,0...) fusion(f32[40]{0:T(128)S(1)} %and_convert_fusion, ...), kind=kLoop, calls=%fused_computation.60 | loop fusion | flops 6225920 | bytes 18771104 | tf_op jit(solution)/shard_map/mul | solution.py:178
  80.1 0.5 fusion.94
  81.2 0.9 broadcast_multiply_fusion.2
  83.5 1.0 copy-done.8
  84.5 2.8 %subtract_multiply_fusion.1 = f32[16,40,512]{2,1,0:T(8,128)S(1)} fusion(f32[16,40,512]{2,1,0:T(8,128)S(1)} %pad_subtract_fusion.4, f32[15,40,512]{2,1,0:T(8,128)S(1)} %slice.239, f32[16,40,512]{2,1,0:T(8,128)S(1)} %pad_subtract_fusion.5, f32[15,40,512]{2,1,0:T(8,128)S(1)} %slice.236, f32[16,40,512]{2,1,0:T(8,128)S(1)} %pad_subtract_fusion.6, ...), kind=kLoop, calls=%fused_computation.17 | loop fusion | flops 8519680 | bytes 21195936 | tf_op jit(solution)/shard_map/mul | solution.py:179
  87.3 1.7 %fusion.93 = (f32[15,40,512]{2,1,0:T(8,128)}, f32[15,40,512]{2,1,0:T(8,128)}) fusion(f32[16,40,512]{2,1,0:T(8,128)S(1)} %subtract_multiply_fusion.1), kind=kLoop, calls=%fused_computation.155 | loop fusion | bytes 4915200 | tf_op jit(solution)/shard_map/slice | solution.py:92
  89.0 1.8 %fusion.91 = (f32[16,39,512]{2,1,0:T(8,128)}, f32[16,39,512]{2,1,0:T(8,128)}) fusion(f32[16,40,512]{2,1,0:T(8,128)S(1)} %subtract_multiply_fusion.1), kind=kLoop, calls=%fused_computation.153 | loop fusion | bytes 5111808 | tf_op jit(solution)/shard_map/slice | solution.py:92
  90.8 2.0 %fusion.89 = (f32[16,40,511]{2,1,0:T(8,128)}, f32[16,40,511]{2,1,0:T(8,128)}) fusion(f32[16,40,512]{2,1,0:T(8,128)S(1)} %subtract_multiply_fusion.1), kind=kLoop, calls=%fused_computation.151 | loop fusion | bytes 5232640 | tf_op jit(solution)/shard_map/slice | solution.py:86
  92.8 5.0 %multiply_subtract_fusion.4 = (f32[16,40,512]{2,1,0:T(8,128)S(1)}, f32[16,40,512]{2,1,0:T(8,128)S(1)}, f32[16,40,512]{2,1,0:T(8,128)S(1)}, f32[16,40,512]{2,1,0:T(8,128)S(1)}, f32[16,40,512]{2,1,0:T(8,128)S(1)}) fusion(f32[16,40,512]{2,1,0:T(8,128)S(1)} %get-tuple-element.50, f32[16,39,512]{2,1,0:T(8,128)} %get-tuple-element.32, ...), kind=kLoop, calls=%fused_computation.15 | loop fusion | flops 7864320 | bytes 19426464 | tf_op jit(solution)/shard_map/sub | solution.py:178
  97.8 1.2 %slice.258 = f32[15,40,512]{2,1,0:T(8,128)} slice(f32[16,40,512]{2,1,0:T(8,128)S(1)} %get-tuple-element.16), slice={[1:16], [0:40], [0:512]} | slice | bytes 2457600 | tf_op jit(solution)/shard_map/slice | solution.py:86
  99.3 1.5 %slice.255 = f32[16,40,511]{2,1,0:T(8,128)} slice(f32[16,40,512]{2,1,0:T(8,128)S(1)} %get-tuple-element.22), slice={[0:16], [0:40], [1:512]} | slice | bytes 2616320 | tf_op jit(solution)/shard_map/slice | solution.py:86
  100.8 0.8 copy-done.3
  101.6 3.4 %multiply_subtract_fusion.2 = (f32[16,40,512]{2,1,0:T(8,128)S(1)}, f32[16,40,512]{2,1,0:T(8,128)S(1)}, f32[16,40,512]{2,1,0:T(8,128)S(1)}) fusion(f32[16,40,512]{2,1,0:T(8,128)S(1)} %get-tuple-element.16, f32[16,40,511]{2,1,0:T(8,128)S(1)} %slice.252, f32[40]{0:T(128)S(1)} %and_convert_fusion, f32[16,40,512]{2,1,0:T(8,128)S(1)} %get-tuple-element.48, ...), kind=kLoop, calls=%fused_computation.13 | loop fusion | flops 8847360 | bytes 16865440 | tf_op jit(solution)/shard_map/sub | solution.py:178
  108.0 2.1 %multiply_add_fusion = f32[16,40,512]{2,1,0:T(8,128)S(1)} fusion(f32[16,40,512]{2,1,0:T(8,128)S(1)} %pad_subtract_fusion.3, f32[16,39,512]{2,1,0:T(8,128)S(1)} %bitcast.76, f32[15,40,512]{2,1,0:T(8,128)S(1)} %get-tuple-element.35, f32[16,40,512]{2,1,0:T(8,128)S(1)} %get-tuple-element.23, f32[15,40,512]{2,1,0:T(8,128)S(1)} %get-tuple-element.34, ...), kind=kLoop, calls=%fused_computation.11 | loop fusion | flops 4587520 | bytes 15461376 | tf_op jit(solution)/shard_map/add | solution.py:121
  110.0 1.9 %fusion.6 = f32[16,32,512]{2,1,0:T(8,128)} fusion(f32[16,40,512]{2,1,0:T(8,128)S(1)} %get-tuple-element.55, f32[16,40,512]{2,1,0:T(8,128)S(1)} %subtract_multiply_fusion.1, f32[16,40,512]{2,1,0:T(8,128)S(1)} %pad_subtract_fusion, f32[16,40,512]{2,1,0:T(8,128)S(1)} %subtract_multiply_fusion, f32[16,40,512]{2,1,0:T(8,128)S(1)} %multiply_add_fusion, ...), kind=kLoop, calls=%fused_computation.43 | loop fusion | flops 2097152 | bytes 6291584 | tf_op jit(solution)/shard_map/mul | solution.py:179
  (60 shorter events, 8.9 us)
Async XLA Ops:
  0.0 14.6 %copy-start.10 = (s32[48]{0:T(128)S(1)}, s32[48]{0:T(128)}, u32[]{:S(2)}) copy-start(s32[48]{0:T(128)} %param.6) | copy-start | bytes 580
  0.0 14.6 %copy-start.11 = (s32[48]{0:T(128)S(1)}, s32[48]{0:T(128)}, u32[]{:S(2)}) copy-start(s32[48]{0:T(128)} %param.5) | copy-start | bytes 580
  0.0 15.2 %collective-permute-start = (bf16[3,256,256]{2,1,0:T(8,128)(2,1)}, bf16[3,256,256]{2,1,0:T(8,128)(2,1)S(1)}, u32[]{:S(2)}, u32[]{:S(2)}) collective-permute-start(bf16[3,256,256]{2,1,0:T(8,128)(2,1)} %param.4), channel_id=1, source_target_pairs={{0,1},{1,2},{2,3},{3,4},{4,5},{5,6},{6,7},{7,8},{8,9},{9,10},{10,1... | collective-permute-start | bytes 1179656 | tf_op jit(solution)/shard_map/ppermute | solution.py:22
  2.6 12.7 %collective-permute-start.1 = (bf16[3,256,256]{2,1,0:T(8,128)(2,1)}, bf16[3,256,256]{2,1,0:T(8,128)(2,1)S(1)}, u32[]{:S(2)}, u32[]{:S(2)}) collective-permute-start(bf16[3,256,256]{2,1,0:T(8,128)(2,1)} %param.4), channel_id=1, source_target_pairs={{1,0},{2,1},{3,2},{4,3},{5,4},{6,5},{7,6},{8,7},{9,8},{10,9},{11,1... | collective-permute-start | bytes 1179656 | tf_op jit(solution)/shard_map/ppermute | solution.py:24
  12.9 2.4 %copy-start.9 = (bf16[3,256,256]{2,1,0:T(8,128)(2,1)S(1)}, bf16[3,256,256]{2,1,0:T(8,128)(2,1)}, u32[]{:S(2)}) copy-start(bf16[3,256,256]{2,1,0:T(8,128)(2,1)} %param.4) | copy-start | bytes 1179652
  44.4 25.8 %all-to-all-start = ((bf16[1,16,40,512]{3,2,0,1:T(8,128)(2,1)}), bf16[1,16,40,512]{3,2,0,1:T(8,128)(2,1)S(1)}, u32[]{:S(2)}, u32[]{:S(2)}) async-start(bf16[1,16,40,512]{3,2,0,1:T(8,128)(2,1)} %pad_maximum_fusion.1), calls=%async_computation | async-start | bytes 1310720 | tf_op jit(solution)/shard_map/all_to_all | solution.py:160
  70.2 0.8 copy-start.6
  74.0 1.3 %copy-start.7 = (bf16[1,16,40,512]{3,2,0,1:T(8,128)(2,1)S(1)}, bf16[1,16,40,512]{3,2,0,1:T(8,128)(2,1)}, u32[]{:S(2)}) copy-start(bf16[1,16,40,512]{3,2,0,1:T(8,128)(2,1)} %copy-done.6) | copy-start | bytes 1966084
  79.2 2.0 %copy-start.4 = (f32[15,40,512]{2,1,0:T(8,128)}, f32[15,40,512]{2,1,0:T(8,128)S(1)}, u32[]{:S(2)}) copy-start(f32[15,40,512]{2,1,0:T(8,128)S(1)} %slice.237) | copy-start | bytes 3686404
  79.7 1.6 %copy-start = (f32[16,40,511]{2,1,0:T(8,128)}, f32[16,40,511]{2,1,0:T(8,128)S(1)}, u32[]{:S(2)}) copy-start(f32[16,40,511]{2,1,0:T(8,128)S(1)} %slice.231) | copy-start | bytes 3924484
  80.1 1.1 %copy-start.2 = (f32[16,40,511]{2,1,0:T(8,128)}, f32[16,40,511]{2,1,0:T(8,128)S(1)}, u32[]{:S(2)}) copy-start(f32[16,40,511]{2,1,0:T(8,128)S(1)} %slice.234) | copy-start | bytes 3924484
  83.4 1.1 copy-start.8
  98.9 1.9 %copy-start.5 = (f32[15,40,512]{2,1,0:T(8,128)S(1)}, f32[15,40,512]{2,1,0:T(8,128)}, u32[]{:S(2)}) copy-start(f32[15,40,512]{2,1,0:T(8,128)} %copy-done.4) | copy-start | bytes 3686404
  99.3 1.5 %copy-start.1 = (f32[16,40,511]{2,1,0:T(8,128)S(1)}, f32[16,40,511]{2,1,0:T(8,128)}, u32[]{:S(2)}) copy-start(f32[16,40,511]{2,1,0:T(8,128)} %copy-done) | copy-start | bytes 3924484
  99.3 2.3 %copy-start.3 = (f32[16,40,511]{2,1,0:T(8,128)S(1)}, f32[16,40,511]{2,1,0:T(8,128)}, u32[]{:S(2)}) copy-start(f32[16,40,511]{2,1,0:T(8,128)} %copy-done.2) | copy-start | bytes 3924484
where the time goes:
time: 113 us; the launch traced here: 112 us
  other arithmetic  41.5 us (37%)
  local copies, waits for them, and re-layouts  29.6 us (26%)
  waiting for transfers between devices  16.5 us (15%)
  starting transfers between devices  13.1 us (12%)
  matrix products  10.9 us (10%)
    all_to_all x1, waiting for transfers between devices, shards(): lax.all_to_all(windows, 'tm', split_axis=1, concat_axis=0, tiled=True)  16.5 us
    slice x15, local copies, waits for them, and re-layouts, shift_ahead(): lax.slice_in_dim(field, 1, count, axis=axis)  10.7 us
    all_to_all x1, starting transfers between devices, shards(): lax.all_to_all(windows, 'tm', split_axis=1, concat_axis=0, tiled=True)  9.25 us
    convert_element_type x1, other arithmetic, half_table(): return (parity / (coarse * jnp.tan(angle_arg))).astype(jnp.bfloat16)  9.02 us
    sub x2, other arithmetic, shards(): 2.0 * new_dual - dual  8.4 us
    reduce_sum x1, other arithmetic, shards(): weighted.reshape(out_count + 2, 3, fine_width, fine_width).sum(axis=1)  6.88 us
    dot_general x1, matrix products, weighted_frames(): jnp.einsum('fij,kj->fik', rows_done, spread, preferred_element_type=jnp.f...  6.2 us
    reshape x1, local copies, waits for them, and re-layouts, weighted_frames(): jnp.stack([raw_block, odd_rows], axis=2)  6.12 us
  transfers between devices with their start and end apart: 3, of which 1 were waited for; matrix products, arithmetic and copies ran while one was open for 10% of the time, Pallas kernels for 0%

commit v1 on v0

v1 whole, which is shorter than its diff:
```python
import jax
import jax.numpy as jnp
import numpy as np
from jax import lax
from jax.experimental import pallas as pl
from jax.experimental.pallas import tpu as pltpu
from jax.sharding import PartitionSpec as P

SWEEPS = 2
STEP_SIZE = 0.01
THRESHOLD = 2.0
REACH = 2 * SWEEPS
LANES = 128
SUBLANES = 8


def half_table(coarse):
    offset = np.arange(coarse)[:, None] - np.arange(coarse)[None, :]
    parity = (1.0 - 2.0 * (offset % 2)).astype(np.float32)
    angle_arg = np.float32(np.pi) * (offset.astype(np.float32) + np.float32(0.5)) / np.float32(coarse)
    return (parity / (np.float32(coarse) * np.tan(angle_arg))).astype(jnp.bfloat16)


def wiener_table(width):
    distance = np.abs(np.arange(width)[:, None] - np.arange(width)[None, :])
    distance = np.minimum(distance, width - distance)
    taps = np.float32(-0.01) * np.power(np.float32(0.98), (distance - 1).astype(np.float32))
    return np.where(distance == 0, np.float32(1.0), taps).astype(jnp.bfloat16)


def split_order(width):
    return np.concatenate([np.arange(0, width, 2), np.arange(1, width, 2)])


def window_rows_of(block_rows):
    rows = block_rows + 2 * REACH
    major = rows // SUBLANES
    stored = np.arange(rows)
    return (stored % SUBLANES) * major + stored // SUBLANES


def row_filter(wiener, blocks, block_rows):
    fine = wiener.shape[0]
    row = np.arange(blocks)[:, None] * block_rows - REACH + window_rows_of(block_rows)[None, :]
    valid = (row >= 0) & (row < fine)
    table = wiener[np.clip(row, 0, fine - 1)][:, :, split_order(fine)]
    return np.where(valid[:, :, None], table, np.zeros((), jnp.bfloat16)).reshape(-1, fine)


def dot(a, b, dims=((1,), (0,))):
    return lax.dot_general(a, b, (dims, ((), ())), preferred_element_type=jnp.float32)


def high_low(value):
    high = value.astype(jnp.bfloat16)
    return high, (value - high.astype(jnp.float32)).astype(jnp.bfloat16)


def filter_kernel(angle_ref, phase_ref, shift_ref, raw_ref, half_ref, col_ref, row_ref, out_ref, sum_ref):
    frames, coarse, _ = raw_ref.shape
    fine = 2 * coarse
    first = lax.axis_index("tm") * frames
    half_step = half_ref[...]
    lane = lax.broadcasted_iota(jnp.int32, (SUBLANES, fine), 1)
    line = lax.broadcasted_iota(jnp.int32, (SUBLANES, fine), 0)
    place = jnp.where(lane < coarse, 2 * lane, 2 * (lane - coarse) + 1)
    for f in range(frames):
        angle = angle_ref[first + f]
        phase = phase_ref[first + f]
        shift_y = shift_ref[angle, 0]
        shift_x = shift_ref[angle, 1]
        cycle = lax.rem(jnp.where(line == 0, shift_y, shift_x) * place, fine)
        turn = (3 * cycle - jnp.where(line == 0, 0, phase * fine)).astype(jnp.float32) / (3.0 * fine)
        turn = 2.0 * jnp.pi * turn
        cos_hi, cos_lo = high_low(jnp.cos(turn))
        sin_hi, sin_lo = high_low(jnp.sin(turn))
        scaled_cos = high_low((2.0 / 3.0) * jnp.cos(turn))
        scaled_sin = high_low((-2.0 / 3.0) * jnp.sin(turn))
        third = high_low(jnp.full((1, fine), 1.0 / 3.0, jnp.float32))
        ones = jnp.ones((1, fine), jnp.bfloat16)
        left = jnp.concatenate(
            [cos_hi[0:1], cos_lo[0:1], cos_hi[0:1], sin_hi[0:1], sin_lo[0:1], sin_hi[0:1], ones, ones], axis=0
        )
        right = jnp.concatenate(
            [
                scaled_cos[0][1:2], scaled_cos[0][1:2], scaled_cos[1][1:2],
                scaled_sin[0][1:2], scaled_sin[0][1:2], scaled_sin[1][1:2],
                third[0], third[1],
            ],
            axis=0,
        )
        weight = dot(left, right, ((0,), (0,)))
        raw = raw_ref[f]
        odd_rows = dot(half_step, raw).astype(jnp.bfloat16)
        rows_done = jnp.concatenate([raw, odd_rows], axis=0)
        odd_cols = dot(rows_done, half_step, ((1,), (1,)))
        even_part = weight[:, :coarse] * rows_done.astype(jnp.float32)
        odd_part = weight[:, coarse:] * odd_cols
        if f == 0:
            sum_ref[:, :coarse] = even_part
            sum_ref[:, coarse:] = odd_part
        else:
            sum_ref[:, :coarse] += even_part
            sum_ref[:, coarse:] += odd_part
    summed = sum_ref[...].astype(jnp.bfloat16)
    filtered = dot(summed, col_ref[...], ((1,), (1,))).astype(jnp.bfloat16)
    windows = dot(row_ref[...], filtered)
    out_ref[...] = windows.reshape(out_ref.shape).astype(jnp.bfloat16)


def ahead_y(parts):
    return [jnp.concatenate([v[SUBLANES:], pltpu.roll(v[:SUBLANES], SUBLANES - 1, 0)], axis=0) for v in parts]


def behind_y(parts):
    return [jnp.concatenate([pltpu.roll(v[-SUBLANES:], 1, 0), v[:-SUBLANES]], axis=0) for v in parts]


def ahead_x(parts, last_lane):
    turned = [pltpu.roll(v, LANES - 1, 1) for v in parts]
    following = turned[1:] + [jnp.zeros_like(parts[0])]
    return [jnp.where(last_lane, n, v) for v, n in zip(turned, following)]


def behind_x(parts, edge, first_lane):
    turned = [pltpu.roll(v, 1, 1) for v in parts]
    before = [edge] + turned[:-1]
    return [jnp.where(first_lane, p, v) for v, p in zip(turned, before)]


def add(a, b):
    return [x + y for x, y in zip(a, b)]


def sub(a, b):
    return [x - y for x, y in zip(a, b)]


def scale(a, factor):
    return [x * factor for x in a]


def clip(a, bound):
    return [jnp.minimum(jnp.maximum(x, -bound), bound) for x in a]


def denoise_kernel(window_ref, out_ref, guide_ref, first_ref, xx_ref, yy_ref, xy_ref, xt_ref, yt_ref, tt_ref,
                   lines_ref):
    count, rows, fine = window_ref.shape
    block_rows = rows - 2 * REACH
    major = rows // SUBLANES
    columns = fine // LANES
    blocks = [pl.ds(c * LANES, LANES) for c in range(columns)]
    lane = lax.broadcasted_iota(jnp.int32, (rows, LANES), 1)
    first_lane = lane == 0
    last_lane = lane == LANES - 1
    stored = lax.broadcasted_iota(jnp.int32, (rows, LANES), 0)
    image_row = (
        lax.axis_index("tm") * block_rows - REACH
        + lax.rem(stored, SUBLANES) * major + lax.div(stored, SUBLANES)
    )
    valid = ((image_row >= 0) & (image_row < fine)).astype(jnp.float32)
    twice_valid = 2.0 * valid

    def load(ref, t):
        return [ref[t, :, b] for b in blocks]

    def store(ref, t, parts):
        for b, v in zip(blocks, parts):
            ref[t, :, b] = v

    zero = [jnp.zeros((rows, LANES), jnp.float32)] * columns
    store(guide_ref, count, zero)
    store(guide_ref, count + 1, zero)
    store(first_ref, count, zero)
    store(first_ref, count + 1, zero)

    def window(t):
        return [window_ref[t, :, b].astype(jnp.float32) for b in blocks]

    store(guide_ref, 0, add(window(0), window(1)))
    store(guide_ref, count - 1, add(window(count - 2), window(count - 1)))

    @pl.loop(1, count - 1)
    def _(t):
        store(guide_ref, t, add(add(window(t - 1), window(t)), window(t + 1)))

    def curve_t(ref, t):
        here, after, beyond = load(ref, t), load(ref, t + 1), load(ref, t + 2)
        return sub(add(here, beyond), scale(after, 2.0))

    def sweep(ref, finish, duals):
        def settle(term, dual_ref, t, bound):
            if duals:
                dual = load(dual_ref, t)
                fresh = clip(add(term, dual), bound)
                return sub(scale(fresh, 2.0), dual)
            fresh = clip(term, bound)
            store(dual_ref, t, fresh)
            return fresh

        def step(t, carried):
            last_xt, last_yt, last_tt, this_tt = carried
            here, after = load(ref, t), load(ref, t + 1)
            rise_t = sub(after, here)
            bound = jnp.where(t + 1 < count, THRESHOLD, 0.0)
            next_tt = settle(curve_t(ref, t), tt_ref, t + 1, bound)

            rise_x = sub(ahead_x(here, last_lane), here)
            carry_xx = settle(sub(rise_x, behind_x(rise_x, here[0], first_lane)), xx_ref, t, THRESHOLD)
            flow_x = sub(ahead_x(carry_xx, last_lane), carry_xx)

            rise_y = sub(ahead_y(here), here)
            curve_y = [v * valid for v in sub(rise_y, behind_y(rise_y))]
            carry_yy = settle(curve_y, yy_ref, t, THRESHOLD)
            flow_y = sub(ahead_y(carry_yy), carry_yy)

            rise_y = [v * twice_valid for v in rise_y]
            carry_xy = settle(sub(ahead_x(rise_y, last_lane), rise_y), xy_ref, t, 2.0 * THRESHOLD)
            flow_x = add(flow_x, sub(carry_xy, behind_y(carry_xy)))

            twice_t = scale(rise_t, 2.0)
            carry_xt = settle(sub(ahead_x(twice_t, last_lane), twice_t), xt_ref, t, 2.0 * THRESHOLD)
            flow_x = add(flow_x, sub(carry_xt, last_xt))

            bend = [v * twice_valid for v in sub(ahead_y(rise_t), rise_t)]
            carry_yt = settle(bend, yt_ref, t, 2.0 * THRESHOLD)
            flow_y = add(flow_y, sub(carry_yt, last_yt))

            total = add(
                sub(flow_x, behind_x(flow_x, carry_xx[0], first_lane)), sub(flow_y, behind_y(flow_y))
            )
            curve = sub(add(next_tt, last_tt), scale(this_tt, 2.0))
            finish(t, here, add(total, curve))
            return carry_xt, carry_yt, this_tt, next_tt

        head = sub(load(ref, 1), scale(load(ref, 0), 2.0))
        first_tt = settle(head, tt_ref, 0, THRESHOLD)
        lax.fori_loop(0, count, step, (zero, zero, zero, first_tt))

    def finish_first(t, here, total):
        update = [(v - (2.0 * STEP_SIZE) * s) * valid for v, s in zip(here, total)]
        store(first_ref, t, update)

    def finish_last(t, here, total):
        for c, (v, s, g) in enumerate(zip(here, total, load(guide_ref, t))):
            update = v - STEP_SIZE * ((v - g) + s)
            for j in range(major):
                lines_ref[c, pl.ds(j, SUBLANES, stride=major), :] = update[j * SUBLANES:(j + 1) * SUBLANES]
            out_ref[t, :, blocks[c]] = lines_ref[c, pl.ds(REACH, block_rows), :]

    sweep(guide_ref, finish_first, False)
    sweep(first_ref, finish_last, True)


def shards(raw_frames, angle_index, phase_index, band_shift):
    raw_count, coarse, _ = raw_frames.shape
    fine = 2 * coarse
    tm_count = lax.axis_size("tm")
    block_rows = fine // tm_count
    window_rows = block_rows + 2 * REACH
    wiener = wiener_table(fine)
    half_step = half_table(coarse)
    col_filter = wiener[:, split_order(fine)]
    row_windows = row_filter(wiener, tm_count, block_rows)
    scalar = pl.BlockSpec(memory_space=pltpu.SMEM)
    vector = pl.BlockSpec(memory_space=pltpu.VMEM)
    windows = pl.pallas_call(
        filter_kernel,
        out_shape=jax.ShapeDtypeStruct((tm_count, window_rows, fine), jnp.bfloat16),
        in_specs=[scalar] * 3 + [vector] * 4,
        out_specs=vector,
        scratch_shapes=[pltpu.VMEM((fine, fine), jnp.float32)],
        name="filter_group",
    )(angle_index, phase_index, band_shift, raw_frames, half_step, col_filter, row_windows)
    received = lax.all_to_all(windows, "tm", split_axis=0, concat_axis=0, tiled=True)

    def field(extra):
        return pltpu.VMEM((tm_count + extra, window_rows, fine), jnp.float32)

    return pl.pallas_call(
        denoise_kernel,
        out_shape=jax.ShapeDtypeStruct((tm_count, block_rows, fine), jnp.float32),
        in_specs=[vector],
        out_specs=vector,
        scratch_shapes=[
            field(2), field(2), field(0), field(0), field(0), field(0), field(0), field(1),
            pltpu.VMEM((fine // LANES, window_rows, LANES), jnp.float32),
        ],
        name="denoise_rows",
    )(received)


def solution(mesh):
    return jax.shard_map(
        shards,
        mesh=mesh,
        in_specs=(P(("grp", "tm"), None, None), P("grp"), P("grp"), P("grp", None)),
        out_specs=P("grp", "tm", None),
        check_vma=False,
    )
```

time: 113 us -> 45.1 us (0.40)
  other arithmetic: 41.5 us -> 0 us
  local copies, waits for them, and re-layouts: 29.6 us -> 1.35 us
  blocking collectives: 0 us -> 25.8 us
  Pallas kernels: 0 us -> 17.6 us
  waiting for transfers between devices: 16.5 us -> 0 us
  starting transfers between devices: 13.1 us -> 0 us
  matrix products: 10.9 us -> 0 us
    all_to_all x0 -> x1, blocking collectives: none -> 25.8 us  [shards(): lax.all_to_all(windows, 'tm', split_axis=0, concat_axis=0, tiled=True)]
    pallas_call x0 -> x2, Pallas kernels: none -> 17.6 us  [the longest x1 13.6 us: shards(): pl.pallas_call(denoise_kernel, out_shape=jax.ShapeDtypeStruct((tm_count,...]
    all_to_all x1 -> x0, waiting for transfers between devices: 16.5 us -> none  [shards(): lax.all_to_all(windows, 'tm', split_axis=1, concat_axis=0, tiled=True)]
    slice x25 -> x0, local copies, waits for them, and re-layouts: 16.2 us -> none  [the longest x15 10.7 us: shift_ahead(): lax.slice_in_dim(field, 1, count, axis=axis)]
    dot_general x3 -> x0, matrix products: 10.9 us -> none  [the longest x1 6.2 us: weighted_frames(): jnp.einsum('fij,kj->fik', rows_done, spread, preferred_element_type=jnp.f...]
    sub x9 -> x0, other arithmetic: 10.9 us -> none  [the longest x2 8.4 us: shards(): 2.0 * new_dual - dual]
    mul x6 -> x0, other arithmetic: 9.81 us -> none  [the longest x2 4.73 us: shards(): (estimate - STEP_SIZE * (estimate - guide_field + adjoint_sum(carried)))...]
    convert_element_type x4 -> x0, other arithmetic: 9.58 us -> none  [the longest x1 9.02 us: half_table(): return (parity / (coarse * jnp.tan(angle_arg))).astype(jnp.bfloat16)]
  transfers between devices with their start and end apart: 3 -> 0, of which waited for: 1 -> 0; matrix products, arithmetic and copies ran while one was open for 10% -> 0% of each run, Pallas kernels for 0% -> 0%
where the time goes in v1:
time: 45.1 us; the launch traced here: 44.8 us
  blocking collectives  25.8 us (57%)
  Pallas kernels  17.6 us (39%)
  local copies, waits for them, and re-layouts  1.35 us (3%)
    all_to_all x1, blocking collectives, shards(): lax.all_to_all(windows, 'tm', split_axis=0, concat_axis=0, tiled=True)  25.8 us
    pallas_call x1, Pallas kernels, shards(): pl.pallas_call(denoise_kernel, out_shape=jax.ShapeDtypeStruct((tm_count,...  13.6 us
    pallas_call x1, Pallas kernels, shards(): pl.pallas_call(filter_kernel, out_shape=jax.ShapeDtypeStruct((tm_count, w...  4.06 us
    unnamed x1, local copies, waits for them, and re-layouts  1.35 us

profile of v1, /device:TPU:0, one launch (start us, length us, event | category | flops | bytes accessed | tf_op | source)
XLA Modules:
  0.0 44.8 jit_solution(7216705423909656986)
XLA Ops:
  0.0 1.4 %copy.8.shift_ref = s32[3,2]{1,0:T(4,128)} copy(s32[3,2]{0,1:T(2,128)} %param.10) | data formatting | bytes 48 | tf_op args[3]
  1.4 4.1 %filter_group.1 = bf16[16,40,512]{2,1,0:T(8,128)(2,1)} custom-call(s32[48]{0:T(128)} %angle_ref.1, s32[48]{0:T(128)} %phase_ref.1, s32[3,2]{1,0:T(4,128)} %copy.8.shift_ref, bf16[3,256,256]{2,1,0:T(8,128)(2,1)} %raw_ref.1, bf16[256,256]{1,0:T(8,128)(2,1)} %constant.6.clone.half_ref, bf16[512,512]{1,0:T(8,128)(2,1)} %constant.7.clone.col_ref, ...), custom_call_target="tpu_custom_call" | custom-call | tf_op jit(solution)/shard_map/filter_group/pallas_call | solution.py:268
  5.4 25.8 %all_to_all.5.window_ref = bf16[16,40,512]{2,1,0:T(8,128)(2,1)} all-to-all(bf16[16,40,512]{2,1,0:T(8,128)(2,1)} %filter_group.1), channel_id=1, replica_groups=mesh['grp'=2,'tm'=16] {'tm'}, dimensions={0} | all-to-all | bytes 1310720 | tf_op jit(solution)/shard_map/all_to_all | solution.py:276
  31.2 13.6 %denoise_rows.1 = f32[16,32,512]{2,1,0:T(8,128)} custom-call(bf16[16,40,512]{2,1,0:T(8,128)(2,1)} %all_to_all.5.window_ref), custom_call_target="tpu_custom_call" | custom-call | tf_op jit(solution)/shard_map/denoise_rows/pallas_call | solution.py:281

commit v2 on v1

v2 whole, which is shorter than its diff:
```python
import jax
import jax.numpy as jnp
import numpy as np
from jax import lax
from jax.experimental import pallas as pl
from jax.experimental.pallas import tpu as pltpu
from jax.sharding import PartitionSpec as P

SWEEPS = 2
STEP_SIZE = 0.01
THRESHOLD = 2.0
REACH = 2 * SWEEPS
LANES = 128
SUBLANES = 8


def half_table(coarse):
    offset = np.arange(coarse)[:, None] - np.arange(coarse)[None, :]
    parity = (1.0 - 2.0 * (offset % 2)).astype(np.float32)
    angle_arg = np.float32(np.pi) * (offset.astype(np.float32) + np.float32(0.5)) / np.float32(coarse)
    return (parity / (np.float32(coarse) * np.tan(angle_arg))).astype(jnp.bfloat16)


def wiener_table(width):
    distance = np.abs(np.arange(width)[:, None] - np.arange(width)[None, :])
    distance = np.minimum(distance, width - distance)
    taps = np.float32(-0.01) * np.power(np.float32(0.98), (distance - 1).astype(np.float32))
    return np.where(distance == 0, np.float32(1.0), taps).astype(jnp.bfloat16)


def split_order(width):
    return np.concatenate([np.arange(0, width, 2), np.arange(1, width, 2)])


def window_rows_of(block_rows):
    rows = block_rows + 2 * REACH
    major = rows // SUBLANES
    stored = np.arange(rows)
    return (stored % SUBLANES) * major + stored // SUBLANES


def columns_of(fine):
    stored = np.arange(fine)
    return (stored % LANES) * (fine // LANES) + stored // LANES


def row_filter(wiener, blocks, block_rows):
    fine = wiener.shape[0]
    row = np.arange(blocks)[:, None] * block_rows - REACH + window_rows_of(block_rows)[None, :]
    valid = (row >= 0) & (row < fine)
    table = wiener[np.clip(row, 0, fine - 1)][:, :, split_order(fine)]
    return np.where(valid[:, :, None], table, np.zeros((), jnp.bfloat16)).reshape(-1, fine)


def dot(a, b, dims=((1,), (0,))):
    return lax.dot_general(a, b, (dims, ((), ())), preferred_element_type=jnp.float32)


def high_low(value):
    high = value.astype(jnp.bfloat16)
    return high, (value - high.astype(jnp.float32)).astype(jnp.bfloat16)


def filter_kernel(angle_ref, phase_ref, shift_ref, raw_ref, half_ref, col_ref, row_ref, out_ref, sum_ref):
    frames, coarse, _ = raw_ref.shape
    fine = 2 * coarse
    first = lax.axis_index("tm") * frames
    half_step = half_ref[...]
    lane = lax.broadcasted_iota(jnp.int32, (SUBLANES, fine), 1)
    line = lax.broadcasted_iota(jnp.int32, (SUBLANES, fine), 0)
    place = jnp.where(lane < coarse, 2 * lane, 2 * (lane - coarse) + 1)
    for f in range(frames):
        angle = angle_ref[first + f]
        phase = phase_ref[first + f]
        shift_y = shift_ref[0, angle]
        shift_x = shift_ref[1, angle]
        cycle = lax.rem(jnp.where(line == 0, shift_y, shift_x) * place, fine)
        turn = (3 * cycle - jnp.where(line == 0, 0, phase * fine)).astype(jnp.float32) / (3.0 * fine)
        turn = 2.0 * jnp.pi * turn
        cos_hi, cos_lo = high_low(jnp.cos(turn))
        sin_hi, sin_lo = high_low(jnp.sin(turn))
        scaled_cos = high_low((2.0 / 3.0) * jnp.cos(turn))
        scaled_sin = high_low((-2.0 / 3.0) * jnp.sin(turn))
        third = high_low(jnp.full((1, fine), 1.0 / 3.0, jnp.float32))
        ones = jnp.ones((1, fine), jnp.bfloat16)
        left = jnp.concatenate(
            [cos_hi[0:1], cos_lo[0:1], cos_hi[0:1], sin_hi[0:1], sin_lo[0:1], sin_hi[0:1], ones, ones], axis=0
        )
        right = jnp.concatenate(
            [
                scaled_cos[0][1:2], scaled_cos[0][1:2], scaled_cos[1][1:2],
                scaled_sin[0][1:2], scaled_sin[0][1:2], scaled_sin[1][1:2],
                third[0], third[1],
            ],
            axis=0,
        )
        weight = dot(left, right, ((0,), (0,)))
        raw = raw_ref[f]
        odd_rows = dot(half_step, raw).astype(jnp.bfloat16)
        rows_done = jnp.concatenate([raw, odd_rows], axis=0)
        odd_cols = dot(rows_done, half_step, ((1,), (1,)))
        even_part = weight[:, :coarse] * rows_done.astype(jnp.float32)
        odd_part = weight[:, coarse:] * odd_cols
        if f == 0:
            sum_ref[:, :coarse] = even_part
            sum_ref[:, coarse:] = odd_part
        else:
            sum_ref[:, :coarse] += even_part
            sum_ref[:, coarse:] += odd_part
    summed = sum_ref[...].astype(jnp.bfloat16)
    filtered = dot(summed, col_ref[...], ((1,), (1,))).astype(jnp.bfloat16)
    windows = dot(row_ref[...], filtered)
    out_ref[...] = windows.reshape(out_ref.shape).astype(jnp.bfloat16)


def add(a, b):
    return [[x + y for x, y in zip(p, q)] for p, q in zip(a, b)]


def sub(a, b):
    return [[x - y for x, y in zip(p, q)] for p, q in zip(a, b)]


def times(a, factor):
    return [[x * factor for x in p] for p in a]


def by_row(a, factors):
    return [[x * f for x in p] for p, f in zip(a, factors)]


def clip(a, bound):
    return [[jnp.minimum(jnp.maximum(x, -bound), bound) for x in p] for p in a]


def ahead_y(a):
    return a[1:] + [[pltpu.roll(x, SUBLANES - 1, 0) for x in a[0]]]


def behind_y(a):
    return [[pltpu.roll(x, 1, 0) for x in a[-1]]] + a[:-1]


def ahead_x(a, last_lane):
    return [
        p[1:] + [jnp.where(last_lane, 0.0, pltpu.roll(p[0], LANES - 1, 1))] for p in a
    ]


def behind_x(a, first_lane, edge=None):
    return [
        [jnp.where(first_lane, 0.0 if edge is None else edge[j][0], pltpu.roll(p[-1], 1, 1))] + p[:-1]
        for j, p in enumerate(a)
    ]


def denoise_kernel(window_ref, order_ref, out_ref, guide_ref, first_ref, xx_ref, yy_ref, xy_ref, xt_ref, yt_ref, tt_ref,
                   past_ref, curve_ref, lines_ref, turned_ref):
    count, rows, fine = window_ref.shape
    block_rows = rows - 2 * REACH
    major = rows // SUBLANES
    columns = fine // LANES
    tiles = [
        [(pl.ds(j * SUBLANES, SUBLANES), pl.ds(c * LANES, LANES)) for c in range(columns)] for j in range(major)
    ]
    lane = lax.broadcasted_iota(jnp.int32, (SUBLANES, LANES), 1)
    first_lane = lane == 0
    last_lane = lane == LANES - 1
    sublane = lax.broadcasted_iota(jnp.int32, (SUBLANES, LANES), 0)
    top_row = lax.axis_index("tm") * block_rows - REACH
    valid, twice_valid, twice_step = [], [], []
    for j in range(major):
        image_row = top_row + sublane * major + j
        inside = (image_row >= 0) & (image_row < fine)
        valid.append(jnp.where(inside, 1.0, 0.0))
        twice_valid.append(jnp.where(inside, 2.0, 0.0))
        twice_step.append(jnp.where(inside, 2.0 * STEP_SIZE, 0.0))

    def load(ref, t):
        return [[ref[(t, *tile)] for tile in line] for line in tiles]

    def store(ref, t, values):
        for line, p in zip(tiles, values):
            for tile, x in zip(line, p):
                ref[(t, *tile)] = x

    zero = [[jnp.zeros((SUBLANES, LANES), jnp.float32)] * columns] * major

    def window(t):
        parts = [window_ref[t, :, pl.ds(c * LANES, LANES)].astype(jnp.float32) for c in range(columns)]
        return [[v[j * SUBLANES:(j + 1) * SUBLANES] for v in parts] for j in range(major)]

    def close(ref):
        store(ref, count, zero)
        store(ref, count + 1, times(load(ref, count - 1), -1.0))

    store(guide_ref, 0, add(window(0), window(1)))
    store(guide_ref, count - 1, add(window(count - 2), window(count - 1)))
    close(guide_ref)

    def gather(t, carried):
        store(guide_ref, t, add(add(window(t - 1), window(t)), window(t + 1)))
        return carried

    lax.fori_loop(1, count - 1, gather, 0)

    def sweep(ref, finish, duals, before_pair=None):
        def settle(term, dual_ref, t, bound):
            if duals:
                return clip(add(term, load(dual_ref, t)), bound)
            fresh = clip(term, bound)
            store(dual_ref, t, fresh)
            return fresh

        def frame(t):
            here = load(ref, t)
            rise_x = sub(ahead_x(here, last_lane), here)
            fresh_xx = settle(sub(rise_x, behind_x(rise_x, first_lane, here)), xx_ref, t, THRESHOLD)
            flow_x = sub(ahead_x(fresh_xx, last_lane), fresh_xx)
            rise_y = sub(ahead_y(here), here)
            double_rise = by_row(rise_y, twice_valid)
            fresh_xy = settle(sub(ahead_x(double_rise, last_lane), double_rise), xy_ref, t, 2.0 * THRESHOLD)
            flow_x = add(flow_x, sub(fresh_xy, behind_y(fresh_xy)))
            total = sub(flow_x, behind_x(flow_x, first_lane, fresh_xx))

            curve_y = by_row(sub(rise_y, behind_y(rise_y)), valid)
            fresh_yy = settle(curve_y, yy_ref, t, THRESHOLD)
            flow_y = sub(ahead_y(fresh_yy), fresh_yy)
            total = add(total, sub(flow_y, behind_y(flow_y)))

            after = load(ref, t + 1)
            rise_t = sub(after, here)
            twice_t = times(rise_t, 2.0)
            fresh_xt = settle(sub(ahead_x(twice_t, last_lane), twice_t), xt_ref, t, 2.0 * THRESHOLD)
            bend = by_row(sub(ahead_y(rise_t), rise_t), twice_valid)
            fresh_yt = settle(bend, yt_ref, t, 2.0 * THRESHOLD)
            flow_t = add(sub(fresh_xt, behind_x(fresh_xt, first_lane)), sub(fresh_yt, behind_y(fresh_yt)))
            next_tt = settle(sub(sub(load(ref, t + 2), after), rise_t), tt_ref, t + 1, THRESHOLD)
            flow_t = add(flow_t, sub(next_tt, load(curve_ref, 0)))
            total = add(total, sub(flow_t, load(past_ref, 0)))
            store(past_ref, 0, flow_t)
            store(curve_ref, 0, next_tt)
            finish(t, here, total)

        def pair(k, carried):
            if before_pair is not None:
                before_pair(jnp.maximum(k - 1, 0))
            frame(2 * k)
            frame(2 * k + 1)
            return carried

        start = load(ref, 0)
        first_tt = settle(sub(sub(load(ref, 1), start), start), tt_ref, 0, THRESHOLD)
        store(curve_ref, 0, first_tt)
        store(past_ref, 0, first_tt)
        lax.fori_loop(0, count // 2, pair, 0)

    def finish_first(t, here, total):
        store(first_ref, t, sub(here, by_row(total, twice_step)))

    def finish_last(t, here, total):
        change = sub(load(guide_ref, t), here)
        update = sub(add(here, times(change, STEP_SIZE + 0.5)), times(total, 2.0 * STEP_SIZE))
        slot = lax.rem(t, 2) * block_rows
        for c in range(columns):
            for j in range(major):
                lines_ref[c, pl.ds(j, SUBLANES, stride=major), :] = update[j][c]
            high, low = high_low(lines_ref[c, pl.ds(REACH, block_rows), :])
            turned_ref[pl.ds(slot, block_rows), pl.ds(c * LANES, LANES)] = high
            turned_ref[pl.ds(2 * block_rows + slot, block_rows), pl.ds(c * LANES, LANES)] = low

    def reorder(k):
        both = dot(turned_ref[...], order_ref[...])
        both = both[:2 * block_rows] + both[2 * block_rows:]
        out_ref[pl.ds(2 * k, 2)] = both.reshape(2, block_rows, fine)

    sweep(guide_ref, finish_first, False)
    close(first_ref)
    turned_ref[...] = jnp.zeros_like(turned_ref)
    sweep(first_ref, finish_last, True, reorder)
    reorder(count // 2 - 1)


def shards(raw_frames, angle_index, phase_index, band_shift):
    raw_count, coarse, _ = raw_frames.shape
    fine = 2 * coarse
    tm_count = lax.axis_size("tm")
    block_rows = fine // tm_count
    window_rows = block_rows + 2 * REACH
    wiener = wiener_table(fine)
    half_step = half_table(coarse)
    col_filter = wiener[columns_of(fine)][:, split_order(fine)]
    row_windows = row_filter(wiener, tm_count, block_rows)
    order = np.eye(fine, dtype=jnp.bfloat16)[columns_of(fine)]
    scalar = pl.BlockSpec(memory_space=pltpu.SMEM)
    vector = pl.BlockSpec(memory_space=pltpu.VMEM)
    windows = pl.pallas_call(
        filter_kernel,
        out_shape=jax.ShapeDtypeStruct((tm_count, window_rows, fine), jnp.bfloat16),
        in_specs=[scalar] * 3 + [vector] * 4,
        out_specs=vector,
        scratch_shapes=[pltpu.VMEM((fine, fine), jnp.float32)],
        name="filter_group",
    )(angle_index, phase_index, band_shift.T, raw_frames, half_step, col_filter, row_windows)
    received = lax.all_to_all(windows, "tm", split_axis=0, concat_axis=0, tiled=True)

    def field(frames):
        return pltpu.VMEM((frames, window_rows, fine), jnp.float32)

    return pl.pallas_call(
        denoise_kernel,
        out_shape=jax.ShapeDtypeStruct((tm_count, block_rows, fine), jnp.float32),
        in_specs=[vector] * 2,
        out_specs=vector,
        scratch_shapes=[
            field(tm_count + 2), field(tm_count + 2), *[field(tm_count)] * 5, field(tm_count + 1),
            field(1), field(1), pltpu.VMEM((fine // LANES, window_rows, LANES), jnp.float32),
            pltpu.VMEM((4 * block_rows, fine), jnp.bfloat16),
        ],
        name="denoise_rows",
    )(received, order)


def solution(mesh):
    return jax.shard_map(
        shards,
        mesh=mesh,
        in_specs=(P(("grp", "tm"), None, None), P("grp"), P("grp"), P("grp", None)),
        out_specs=P("grp", "tm", None),
        check_vma=False,
    )
```

time: 45.1 us -> 39.1 us (0.87)
  Pallas kernels: 17.6 us -> 13 us
  local copies, waits for them, and re-layouts: 1.35 us -> 0 us
    pallas_call x1, Pallas kernels: 13.6 us -> 8.93 us  [shards(): pl.pallas_call(denoise_kernel, out_shape=jax.ShapeDtypeStruct((tm_count,...]
    unnamed x1 -> x0, local copies, waits for them, and re-layouts: 1.35 us -> none
where the time goes in v2:
time: 39.1 us; the launch traced here: 38.8 us
  blocking collectives  25.8 us (66%)
  Pallas kernels  13 us (33%)
    all_to_all x1, blocking collectives, shards(): lax.all_to_all(windows, 'tm', split_axis=0, concat_axis=0, tiled=True)  25.8 us
    pallas_call x1, Pallas kernels, shards(): pl.pallas_call(denoise_kernel, out_shape=jax.ShapeDtypeStruct((tm_count,...  8.93 us
    pallas_call x1, Pallas kernels, shards(): pl.pallas_call(filter_kernel, out_shape=jax.ShapeDtypeStruct((tm_count, w...  4.07 us

profile of v2, /device:TPU:0, one launch (start us, length us, event | category | flops | bytes accessed | tf_op | source)
XLA Modules:
  0.0 38.8 jit_solution(14893469558634914497)
XLA Ops:
  0.0 4.1 %filter_group.1 = bf16[16,40,512]{2,1,0:T(8,128)(2,1)} custom-call(s32[48]{0:T(128)} %angle_ref.1, s32[48]{0:T(128)} %phase_ref.1, s32[2,3]{1,0:T(2,128)} %bitcast.1, bf16[3,256,256]{2,1,0:T(8,128)(2,1)} %raw_ref.1, bf16[256,256]{1,0:T(8,128)(2,1)} %constant.8.clone.half_ref, bf16[512,512]{1,0:T(8,128)(2,1)} %constant.9.clone.col_ref, ...), custom_call_target="tpu_custom_call" | custom-call | tf_op jit(solution)/shard_map/filter_group/pallas_call | solution.py:297
  4.1 25.8 %all_to_all.5.window_ref = bf16[16,40,512]{2,1,0:T(8,128)(2,1)} all-to-all(bf16[16,40,512]{2,1,0:T(8,128)(2,1)} %filter_group.1), channel_id=1, replica_groups=mesh['grp'=2,'tm'=16] {'tm'}, dimensions={0} | all-to-all | bytes 1310720 | tf_op jit(solution)/shard_map/all_to_all | solution.py:305
  29.9 8.9 %denoise_rows.1 = f32[16,32,512]{2,1,0:T(8,128)} custom-call(bf16[16,40,512]{2,1,0:T(8,128)(2,1)} %all_to_all.5.window_ref, bf16[512,512]{1,0:T(8,128)(2,1)} %constant.11.clone.order_ref), custom_call_target="tpu_custom_call" | custom-call | tf_op jit(solution)/shard_map/denoise_rows/pallas_call | solution.py:310
